TPU v7x, 256 devices: a whole 4x4x8 slice. The times are simulated.
256 devices in a mesh: frames: 4 (over z_hi), states: 64 (over z_lo, y, x, core).
Axes of the slice: x: 4, y: 4, z: 8 (z_hi: 4, z_lo: 2; z = z_hi * 2 + z_lo), core: 2. Of those that a mesh axis runs over, the one named last changes fastest.
Arguments:
- features: bfloat16 [16384, 1024], P('states', 'frames'), may hold values from -10 to 10
- state_ids: int32 [16384, 32], P('states'), may hold values from 0 to 6143, as said below
- weights: float32 [16384, 32], P('states'), may hold values from 0.05 to 1
Outputs:
- means: bfloat16 [6144, 1024], P(None, 'frames')
- precisions: bfloat16 [6144, 1024], P(None, 'frames')
- frame_score: float32 [16384], P('states')
Inputs may be any that keep to these rules, and one draw needn't show every extreme that they name: `state_ids`: each row names 32 different states; every state is named by some row.
All inputs are finite; a program needn't handle non-finite values.
Results may differ from a plain program's by a relative error of at most 0.0034.
Values may be sent and summed in bfloat16 or wider, within the bound.
A program may use at most 128 MiB of HBM per device.

v0:
```python
import jax
import jax.numpy as jnp
from jax import lax
from jax.sharding import PartitionSpec as P

D = 1024
STATE_DEV = 96
variance_floor = 0.25


def copy_for_each(shard, axis):
    copies = jnp.broadcast_to(shard, (lax.axis_size(axis), *shard.shape))
    return lax.all_to_all(copies, axis, split_axis=0, concat_axis=0, tiled=True)


def taken_together(shard, axis):
    everything = copy_for_each(shard, axis)
    return jnp.sum(everything, axis=0)


def refresh(first, second, counts):
    mean_value = first / counts
    variance = jnp.maximum(second / counts - mean_value * mean_value, variance_floor)
    return (mean_value.astype(jnp.bfloat16), (1.0 / variance).astype(jnp.bfloat16))


def per_device(features, state_ids, weights):
    rows_here, local_width = features.shape
    group_size = lax.axis_size("states")
    total_states = STATE_DEV * group_size
    row_index = jnp.arange(rows_here, dtype=jnp.int32)[:, None]
    rounded = weights.astype(jnp.bfloat16)
    posterior = (
        jnp.zeros((rows_here, total_states), jnp.bfloat16).at[row_index, state_ids].add(rounded)
    )
    values = features.astype(jnp.float32)
    squares = (values * values).astype(jnp.bfloat16)
    blocked = posterior.reshape(rows_here, group_size, STATE_DEV)
    routed = lax.all_to_all(blocked, "states", split_axis=1, concat_axis=0, tiled=True)
    routed = routed.reshape(rows_here * group_size, STATE_DEV)
    owned_counts = jnp.sum(routed, axis=0, dtype=jnp.float32)
    piece = lax.all_gather(features, "states", axis=0, tiled=True)
    piece_f = piece.astype(jnp.float32)
    piece_sq = (piece_f * piece_f).astype(jnp.bfloat16)
    joined = jnp.concatenate([piece, piece_sq], axis=1)
    owned_sums = lax.dot_general(
        routed, joined, (((0,), (0,)), ((), ())), preferred_element_type=jnp.float32
    )
    mean_rows, prec_rows = refresh(
        owned_sums[:, :local_width], owned_sums[:, local_width:], owned_counts[:, None]
    )
    packed = lax.all_gather(
        jnp.concatenate([mean_rows, prec_rows], axis=1), "states", axis=0, tiled=True
    )
    means = packed[:, :local_width]
    precisions = packed[:, local_width:]
    mean_f = means.astype(jnp.float32)
    prec_f = precisions.astype(jnp.float32)
    product = (mean_f * prec_f).astype(jnp.bfloat16)
    constant_term = jnp.sum(mean_f * product.astype(jnp.float32) - jnp.log(prec_f), axis=1)
    lookup_table = jnp.concatenate([precisions, product], axis=1)
    weight_f = rounded.astype(jnp.float32)
    blended = jnp.dot(posterior, lookup_table, preferred_element_type=jnp.float32)
    quadratic = jnp.sum(
        squares.astype(jnp.float32) * blended[:, :local_width]
        - 2.0 * values * blended[:, local_width:],
        axis=1,
    )
    quadratic = quadratic + jnp.sum(weight_f * constant_term[state_ids], axis=1)
    summed = taken_together(quadratic, "frames")
    weight_sum = jnp.sum(weight_f, axis=1)
    frame_score = -0.5 * summed / (D * weight_sum)
    return (means, precisions, frame_score)


def solution(mesh):
    return jax.shard_map(
        per_device,
        mesh=mesh,
        in_specs=(P("states", "frames"), P("states", None), P("states", None)),
        out_specs=(P(None, "frames"), P(None, "frames"), P("states")),
        check_vma=False,
    )
```

profile of v0, /device:TPU:1, one launch (start us, length us, event | category | flops | bytes accessed | tf_op | source)
XLA Modules:
  0.0 357.5 jit_solution(10742842729083389817)
XLA Ops:
  7.2 0.0 all-gather.3.cloned.1.call-start
  7.2 0.7 all-gather.3.cloned.1.call-update
  7.9 0.0 all-gather.5.cloned.1.call-start
  7.9 0.9 copy.20
  8.8 0.1 reshape.37
  8.9 0.8 compare_select_fusion
  9.7 0.7 multiply_reduce_fusion
  10.4 0.7 and_reduce_fusion
  11.2 0.1 copy.19
  11.3 0.1 reshape.35
  11.4 57.8 %scatter_custom_fusion = bf16[1572864]{0:T(1024)(128)(2,1)S(1)} fusion(s32[8192]{0:T(1024)S(1)} %reshape.35, bf16[8192]{0:T(1024)(128)(2,1)S(1)} %reshape.37, bf16[]{:T(256)} %constant.9.clone.1), kind=kCustom, calls=%fused_computation.18 | custom fusion | flops 8192 | bytes 3145730
  69.2 4.0 %reshape.20 = bf16[256,64,96]{2,1,0:T(8,128)(2,1)} reshape(bf16[1572864]{0:T(1024)(128)(2,1)S(1)} %scatter_custom_fusion) | data formatting | bytes 6291456 | tf_op jit(solution)/shard_map/reshape | solution.py:38
  73.2 6.5 %copy.21 = bf16[256,64,96]{0,2,1:T(8,128)(2,1)} copy(bf16[256,64,96]{2,1,0:T(8,128)(2,1)} %reshape.20) | data formatting | bytes 6291456 | tf_op jit(solution)/shard_map/reshape | solution.py:38
  79.8 53.9 %all_to_all.21 = bf16[256,64,96]{0,2,1:T(8,128)(2,1)S(1)} all-to-all(bf16[256,64,96]{0,2,1:T(8,128)(2,1)} %copy.21), channel_id=1, replica_groups=mesh['frames'=4,'states'=64] {'states'}, dimensions={1} | all-to-all | bytes 6291456 | tf_op jit(solution)/shard_map/all_to_all | solution.py:39
  133.7 1.9 copy.26
  135.6 0.5 convert_reduce_fusion
  136.2 18.2 %all-gather.3.cloned.1.call-done = bf16[16384,256]{1,0:T(8,128)(2,1)} async-done(((bf16[256,256]{1,0:T(8,128)(2,1)}), bf16[16384,256]{1,0:T(8,128)(2,1)}) %all-gather.3.cloned.1.call-update) | async-done | bytes 8388624 | tf_op jit(solution)/shard_map/all_gather | solution.py:42
  154.3 0.0 copy-start
  154.3 0.0 copy-start.2
  154.3 8.7 %multiply_convert_fusion = bf16[16384,256]{1,0:T(8,128)(2,1)} fusion(bf16[16384,256]{1,0:T(8,128)(2,1)} %all-gather.3.cloned.1.call-done), kind=kLoop, calls=%fused_computation.6 | loop fusion | flops 12582912 | bytes 16777216 | tf_op jit(solution)/shard_map/convert_element_type | solution.py:44
  163.1 0.0 copy-done
  163.1 1.1 copy-done.2
  164.2 8.5 %fusion = f32[96,512]{1,0:T(8,128)S(1)} fusion(bf16[16384,96]{0,1:T(8,128)(2,1)S(1)} %bitcast.16, bf16[16384,256]{1,0:T(8,128)(2,1)} %multiply_convert_fusion, bf16[16384,256]{1,0:T(8,128)(2,1)S(1)} %copy-done), kind=kOutput, calls=%fused_computation.2 | convolution fusion | flops 1644167168 | bytes 20119552 | tf_op jit(solution)/shard_map/dot_general | solution.py:46
  172.7 0.1 fusion.22
  172.8 0.6 pad_maximum_fusion
  173.5 0.0 all-gather.5.cloned.1.call-update
  173.5 2.9 reshape.25
  176.4 0.1 copy.23
  176.5 0.1 reshape.29
  176.6 0.0 copy-start.1
  176.6 108.3 %all-gather.5.cloned.1.call-done = bf16[6144,512]{1,0:T(8,128)(2,1)} async-done(((bf16[96,512]{1,0:T(8,128)(2,1)}), bf16[6144,512]{1,0:T(8,128)(2,1)}) %all-gather.5.cloned.1.call-update) | async-done | bytes 6291472 | tf_op jit(solution)/shard_map/all_gather | solution.py:52
  284.9 4.9 %fusion.5 = (f32[6144]{0:T(1024)S(1)}, bf16[6144,256]{1,0:T(8,128)(2,1)S(1)}, bf16[6144,256]{1,0:T(8,128)(2,1)S(1)}, bf16[6144,256]{1,0:T(8,128)(2,1)}) fusion(bf16[6144,512]{1,0:T(8,128)(2,1)} %all-gather.5.cloned.1.call-done), kind=kLoop, calls=%fused_computation.11 | loop fusion | flops 12576768 | bytes 15753216 | tf_op jit(solution)/shard_map/reduce_sum | solution.py:60
  289.8 0.0 copy-start.3
  289.8 0.0 copy-done.1
  289.8 0.0 copy-start.4
  289.8 1.8 fusion.7
  291.6 0.0 copy-done.3
  291.7 0.0 copy-done.4
  291.7 0.1 fusion.16
  291.8 45.5 %gather_fusion = f32[8192]{0:T(1024)S(1)} fusion(f32[6144]{0:T(1024)S(1)} %get-tuple-element.5, s32[8192]{0:T(1024)S(1)} %broadcast_clamp_fusion), kind=kCustom, calls=%fused_computation | custom fusion | bytes 98304 | tf_op jit(solution)/shard_map/gather | solution.py:69
  337.3 0.1 reshape.28
  337.4 0.2 fusion.17
  337.6 12.5 %all_to_all.22 = f32[4,1,256]{2,1,0:T(1,128)S(1)} all-to-all(f32[4,1,256]{2,1,0:T(1,128)S(1)} %broadcast_in_dim.20), channel_id=1, replica_groups=mesh['frames'=4,'states'=64] {'frames'}, dimensions={0} | all-to-all | bytes 8192 | tf_op jit(solution)/shard_map/all_to_all | solution.py:13
  350.1 0.6 multiply_divide_fusion
  (6 shorter events, 0.0 us)
Async XLA Ops:
  7.2 147.2 %all-gather.3.cloned.1.call-start = ((), (), s32[]{:S(2)}) async-start(), calls=%async_computation.2 | async-start | bytes 8519680 | tf_op jit(solution)/shard_map/all_gather | solution.py:42
  7.9 277.0 %all-gather.5.cloned.1.call-start = ((), (), s32[]{:S(2)}) async-start(), calls=%async_computation.3 | async-start | bytes 6389760 | tf_op jit(solution)/shard_map/all_gather | solution.py:52
  154.3 8.7 %copy-start = (bf16[16384,256]{1,0:T(8,128)(2,1)S(1)}, bf16[16384,256]{1,0:T(8,128)(2,1)}, u32[]{:S(2)}) copy-start(bf16[16384,256]{1,0:T(8,128)(2,1)} %all-gather.3.cloned.1.call-done) | copy-start | bytes 25165828
  154.3 9.8 %copy-start.2 = (bf16[12,8,64,256]{3,1,2,0:T(8,128)(2,1)S(1)}, bf16[12,8,64,256]{3,1,2,0:T(8,128)(2,1)}, u32[]{:S(2)}) copy-start(bf16[12,8,64,256]{3,1,2,0:T(8,128)(2,1)} %copy.26) | copy-start | bytes 9437188
  176.6 113.2 %copy-start.1 = (bf16[256,6144]{1,0:T(8,128)(2,1)S(1)}, bf16[256,6144]{1,0:T(8,128)(2,1)}, u32[]{:S(2)}) copy-start(bf16[256,6144]{1,0:T(8,128)(2,1)} %reshape.25) | copy-start | bytes 9437188
  289.8 1.9 copy-start.3
  289.8 1.9 copy-start.4
Sparse Core Ops, SparseCore 0:
  9.8 144.4 all-gather.2
  173.6 111.2 all-gather.4
where the time goes:
time: 358 us
  waiting for transfers between devices  127 us (35%)
  other arithmetic  75.8 us (21%)
  blocking collectives  66.4 us (19%)
  local copies, waits for them, and re-layouts  63.5 us (18%)
  between operations  14.2 us (4%)
  matrix products  10.4 us (3%)
    all_gather x1, waiting for transfers between devices, per_device(): lax.all_gather(jnp.concatenate([mean_rows, prec_rows], axis=1), 'states',...  108 us
    unnamed x4, other arithmetic  59.3 us
    all_to_all x1, blocking collectives, per_device(): lax.all_to_all(blocked, 'states', split_axis=1, concat_axis=0, tiled=True)  53.9 us
    gather x2, local copies, waits for them, and re-layouts, per_device(): quadratic = quadratic + jnp.sum(weight_f * constant_term[state_ids], axis=1)  45.6 us
    all_gather x1, waiting for transfers between devices, per_device(): piece = lax.all_gather(features, 'states', axis=0, tiled=True)  18.2 us
    all_to_all x1, blocking collectives, copy_for_each(): return lax.all_to_all(copies, axis, split_axis=0, concat_axis=0, tiled=True)  12.5 us
    reshape x2, local copies, waits for them, and re-layouts, per_device(): blocked = posterior.reshape(rows_here, group_size, STATE_DEV)  10.5 us
    convert_element_type x1, other arithmetic, per_device(): piece_sq = (piece_f * piece_f).astype(jnp.bfloat16)  8.71 us
  transfers between devices with their start and end apart: 2, of which 2 were waited for; matrix products, arithmetic and copies ran while one was open for 22% of the time, Pallas kernels for 0%

commit v1 on v0

--- a/solution.py
+++ b/solution.py
@@ -49,9 +49,11 @@
     mean_rows, prec_rows = refresh(
         owned_sums[:, :local_width], owned_sums[:, local_width:], owned_counts[:, None]
     )
-    packed = lax.all_gather(
-        jnp.concatenate([mean_rows, prec_rows], axis=1), "states", axis=0, tiled=True
-    )
+    own = jnp.concatenate([mean_rows, prec_rows], axis=1)
+    size = lax.axis_size("states")
+    blocks = jnp.stack([own for _ in range(size)])
+    blocks = lax.all_to_all(blocks, "states", split_axis=0, concat_axis=0)
+    packed = jnp.concatenate(blocks, axis=0)
     means = packed[:, :local_width]
     precisions = packed[:, local_width:]
     mean_f = means.astype(jnp.float32)

time: 358 us -> 346 us (0.966)
  the two profiles are of different devices: /device:TPU:1 before, /device:TPU:8 now
where the time goes in v1:
time: 346 us; the launch traced here: 345 us
  waiting for transfers between devices  104 us (30%)
  other arithmetic  75.3 us (22%)
  blocking collectives  66.9 us (19%)
  local copies, waits for them, and re-layouts  66.8 us (19%)
  between operations  14.2 us (4%)
  matrix products  10.4 us (3%)
  starting transfers between devices  7.26 us (2%)
    all_to_all x1, waiting for transfers between devices, per_device(): blocks = lax.all_to_all(blocks, 'states', split_axis=0, concat_axis=0)  84.1 us
    unnamed x4, other arithmetic  59.3 us
    all_to_all x1, blocking collectives, per_device(): lax.all_to_all(blocked, 'states', split_axis=1, concat_axis=0, tiled=True)  53.7 us
    gather x2, local copies, waits for them, and re-layouts, per_device(): quadratic = quadratic + jnp.sum(weight_f * constant_term[state_ids], axis=1)  45.6 us
    all_gather x1, waiting for transfers between devices, per_device(): piece = lax.all_gather(features, 'states', axis=0, tiled=True)  19.4 us
    all_to_all x1, blocking collectives, copy_for_each(): return lax.all_to_all(copies, axis, split_axis=0, concat_axis=0, tiled=True)  13.2 us
    reshape x2, local copies, waits for them, and re-layouts, per_device(): blocked = posterior.reshape(rows_here, group_size, STATE_DEV)  10.5 us
    convert_element_type x1, other arithmetic, per_device(): piece_sq = (piece_f * piece_f).astype(jnp.bfloat16)  8.71 us
  transfers between devices with their start and end apart: 2, of which 2 were waited for; matrix products, arithmetic and copies ran while one was open for 22% of the time, Pallas kernels for 0%

profile of v1, /device:TPU:8, one launch (start us, length us, event | category | flops | bytes accessed | tf_op | source)
XLA Modules:
  0.0 345.0 jit_solution(125567289840019530)
XLA Ops:
  7.2 0.0 all-gather.2.cloned.1.call-start
  7.2 0.7 all-gather.2.cloned.1.call-update
  7.9 0.9 copy.20
  8.8 0.1 reshape.43
  8.9 0.8 compare_select_fusion
  9.7 0.7 multiply_reduce_fusion
  10.4 0.7 and_reduce_fusion
  11.1 0.1 copy.19
  11.2 0.1 reshape.41
  11.3 57.8 %scatter_custom_fusion = bf16[1572864]{0:T(1024)(128)(2,1)S(1)} fusion(s32[8192]{0:T(1024)S(1)} %reshape.41, bf16[8192]{0:T(1024)(128)(2,1)S(1)} %reshape.43, bf16[]{:T(256)} %constant.9.clone.1), kind=kCustom, calls=%fused_computation.18 | custom fusion | flops 8192 | bytes 3145730
  69.2 4.0 %reshape.25 = bf16[256,64,96]{2,1,0:T(8,128)(2,1)} reshape(bf16[1572864]{0:T(1024)(128)(2,1)S(1)} %scatter_custom_fusion) | data formatting | bytes 6291456 | tf_op jit(solution)/shard_map/reshape | solution.py:38
  73.2 6.5 %copy.21 = bf16[256,64,96]{0,2,1:T(8,128)(2,1)} copy(bf16[256,64,96]{2,1,0:T(8,128)(2,1)} %reshape.25) | data formatting | bytes 6291456 | tf_op jit(solution)/shard_map/reshape | solution.py:38
  79.7 53.7 %all_to_all.26 = bf16[256,64,96]{0,2,1:T(8,128)(2,1)S(1)} all-to-all(bf16[256,64,96]{0,2,1:T(8,128)(2,1)} %copy.21), channel_id=1, replica_groups=mesh['frames'=4,'states'=64] {'states'}, dimensions={1} | all-to-all | bytes 6291456 | tf_op jit(solution)/shard_map/all_to_all | solution.py:39
  133.4 1.9 copy.26
  135.3 0.5 convert_reduce_fusion
  135.9 19.4 %all-gather.2.cloned.1.call-done = bf16[16384,256]{1,0:T(8,128)(2,1)} async-done(((bf16[256,256]{1,0:T(8,128)(2,1)}), bf16[16384,256]{1,0:T(8,128)(2,1)}) %all-gather.2.cloned.1.call-update) | async-done | bytes 8388624 | tf_op jit(solution)/shard_map/all_gather | solution.py:42
  155.2 0.0 copy-start
  155.2 0.0 copy-start.2
  155.2 8.7 %multiply_convert_fusion = bf16[16384,256]{1,0:T(8,128)(2,1)} fusion(bf16[16384,256]{1,0:T(8,128)(2,1)} %all-gather.2.cloned.1.call-done), kind=kLoop, calls=%fused_computation.6 | loop fusion | flops 12582912 | bytes 16777216 | tf_op jit(solution)/shard_map/convert_element_type | solution.py:44
  163.9 0.0 copy-done
  163.9 1.1 copy-done.2
  165.0 8.5 %fusion = f32[96,512]{1,0:T(8,128)S(1)} fusion(bf16[16384,96]{0,1:T(8,128)(2,1)S(1)} %bitcast.17, bf16[16384,256]{1,0:T(8,128)(2,1)} %multiply_convert_fusion, bf16[16384,256]{1,0:T(8,128)(2,1)S(1)} %copy-done), kind=kOutput, calls=%fused_computation.2 | convolution fusion | flops 1644167168 | bytes 20119552 | tf_op jit(solution)/shard_map/dot_general | solution.py:46
  173.6 0.1 fusion.22
  173.7 3.4 stack.2
  177.1 7.2 %all-to-all-start.1 = ((bf16[64,96,512]{2,1,0:T(8,128)(2,1)}), bf16[64,96,512]{2,1,0:T(8,128)(2,1)}, u32[]{:S(2)}, u32[]{:S(2)}) async-start(bf16[64,96,512]{2,1,0:T(8,128)(2,1)} %stack.2), calls=%async_computation.1 | async-start | bytes 12582912 | tf_op jit(solution)/shard_map/all_to_all | solution.py:55
  184.4 2.8 reshape.31
  187.2 0.1 copy.23
  187.3 0.1 reshape.35
  187.4 84.1 %all-to-all-done.1 = bf16[64,96,512]{2,1,0:T(8,128)(2,1)} async-done(((bf16[64,96,512]{2,1,0:T(8,128)(2,1)}), bf16[64,96,512]{2,1,0:T(8,128)(2,1)}, u32[]{:S(2)}, u32[]{:S(2)}) %all-to-all-start.1) | async-done | bytes 6291488 | tf_op jit(solution)/shard_map/all_to_all | solution.py:55
  271.6 0.0 copy-start.1
  271.6 5.0 %fusion.5 = (f32[6144]{0:T(1024)S(1)}, bf16[6144,256]{1,0:T(8,128)(2,1)S(1)}, bf16[6144,256]{1,0:T(8,128)(2,1)S(1)}, bf16[6144,256]{1,0:T(8,128)(2,1)}) fusion(bf16[6144,512]{1,0:T(8,128)(2,1)} %bitcast.4), kind=kLoop, calls=%fused_computation.11 | loop fusion | flops 12576768 | bytes 15753216 | tf_op jit(solution)/shard_map/reduce_sum | solution.py:62
  276.6 0.0 copy-start.3
  276.6 0.0 copy-done.1
  276.6 0.0 copy-start.4
  276.6 1.8 fusion.7
  278.4 0.0 copy-done.3
  278.4 0.0 copy-done.4
  278.4 0.1 fusion.16
  278.6 45.5 %gather_fusion = f32[8192]{0:T(1024)S(1)} fusion(f32[6144]{0:T(1024)S(1)} %get-tuple-element.5, s32[8192]{0:T(1024)S(1)} %broadcast_clamp_fusion), kind=kCustom, calls=%fused_computation | custom fusion | bytes 98304 | tf_op jit(solution)/shard_map/gather | solution.py:71
  324.1 0.1 reshape.34
  324.2 0.2 fusion.17
  324.4 13.2 %all_to_all.27 = f32[4,1,256]{2,1,0:T(1,128)S(1)} all-to-all(f32[4,1,256]{2,1,0:T(1,128)S(1)} %broadcast_in_dim.20), channel_id=1, replica_groups=mesh['frames'=4,'states'=64] {'frames'}, dimensions={0} | all-to-all | bytes 8192 | tf_op jit(solution)/shard_map/all_to_all | solution.py:13
  337.6 0.6 multiply_divide_fusion
  (7 shorter events, 0.1 us)
Async XLA Ops:
  7.2 148.1 %all-gather.2.cloned.1.call-start = ((), (), s32[]{:S(2)}) async-start(), calls=%async_computation.3 | async-start | bytes 8519680 | tf_op jit(solution)/shard_map/all_gather | solution.py:42
  155.2 8.7 %copy-start = (bf16[16384,256]{1,0:T(8,128)(2,1)S(1)}, bf16[16384,256]{1,0:T(8,128)(2,1)}, u32[]{:S(2)}) copy-start(bf16[16384,256]{1,0:T(8,128)(2,1)} %all-gather.2.cloned.1.call-done) | copy-start | bytes 25165828
  155.2 9.8 %copy-start.2 = (bf16[12,8,64,256]{3,1,2,0:T(8,128)(2,1)S(1)}, bf16[12,8,64,256]{3,1,2,0:T(8,128)(2,1)}, u32[]{:S(2)}) copy-start(bf16[12,8,64,256]{3,1,2,0:T(8,128)(2,1)} %copy.26) | copy-start | bytes 9437188
  177.1 94.4 %all-to-all-start.1 = ((bf16[64,96,512]{2,1,0:T(8,128)(2,1)}), bf16[64,96,512]{2,1,0:T(8,128)(2,1)}, u32[]{:S(2)}, u32[]{:S(2)}) async-start(bf16[64,96,512]{2,1,0:T(8,128)(2,1)} %stack.2), calls=%async_computation.1 | async-start | bytes 12582912 | tf_op jit(solution)/shard_map/all_to_all | solution.py:55
  271.6 5.0 %copy-start.1 = (bf16[256,6144]{1,0:T(8,128)(2,1)S(1)}, bf16[256,6144]{1,0:T(8,128)(2,1)}, u32[]{:S(2)}) copy-start(bf16[256,6144]{1,0:T(8,128)(2,1)} %reshape.31) | copy-start | bytes 9437188
  276.6 1.8 copy-start.3
  276.6 1.8 copy-start.4
Sparse Core Ops, SparseCore 0:
  9.8 145.3 all-gather.1
